TPU v7x, 32 devices: a whole 2x2x4 slice. The times are simulated.
32 devices in a mesh: rep: 2 (over core), exp: 16 (over z, y, x).
Axes of the slice: x: 2, y: 2, z: 4, core: 2. Of those that a mesh axis runs over, the one named last changes fastest.
Arguments:
- attn_out: bfloat16 [4096, 2048], P(('rep', 'exp')), may hold values from -6 to 6
- resid: bfloat16 [4096, 1024], P(('rep', 'exp')), may hold values from -6 to 6
- out_grad: bfloat16 [4096, 1024], P(('rep', 'exp')), may hold values from -6 to 6
- gain: float32 [1024], replicated, may hold values from 0.5 to 1.5
- expert_ids: int32 [4096, 8], P(('rep', 'exp')), may hold values from 0 to 15, all different within a row; in each aligned block of 128 rows (0 to 127, 128 to 255, ...) at most 72 rows name the same one
- gate_vals: float32 [4096, 8], P(('rep', 'exp')), may hold values from 0.03 to 0.5
- w_gate: bfloat16 [16, 1024, 512], P('exp'), may hold values from -0.1875 to 0.1875
- w_up: bfloat16 [16, 1024, 512], P('exp'), may hold values from -0.1875 to 0.1875
- w_down: bfloat16 [16, 512, 1024], P('exp'), may hold values from -0.25 to 0.25
Outputs:
- d_resid: bfloat16 [4096, 1024], P(('rep', 'exp'))
- projection_grad: float32 [2048, 1024], P(('rep', 'exp'))
- gate_grad: float32 [16, 1024, 512], P('exp', None, 'rep')
- up_grad: float32 [16, 1024, 512], P('exp', None, 'rep')
- down_grad: float32 [16, 512, 1024], P('exp', None, 'rep')
Inputs may be any that keep to these rules, and one draw needn't show every extreme that they name: `expert_ids`: each row names 8 different experts. Among the rows of one device no expert is named more than 72 times, a bound that some block reaches.
All inputs are finite; a program needn't handle non-finite values.
Results may differ from a plain program's by a relative error of at most 0.0095.
Values may be sent and summed in bfloat16 or wider, within the bound.
A program may use at most 128 MiB of HBM per device.

v0:
```python
import functools

import jax
import jax.numpy as jnp
from jax import lax
from jax.experimental import pallas as pl
from jax.experimental.pallas import tpu as pltpu
from jax.sharding import PartitionSpec as P

epsilon = 1e-06
MESH = pl.DeviceIdType.MESH


def contract_rows(left, right):
    return lax.dot_general(
        left, right, (((0,), (0,)), ((), ())), preferred_element_type=jnp.float32
    )


def contract_last(left, right):
    return lax.dot_general(
        left, right, (((1,), (1,)), ((), ())), preferred_element_type=jnp.float32
    )


def grid_of(owners):
    inner = 2 if owners % 2 == 0 else 1
    middle = 2 if owners % 4 == 0 else 1
    return owners // (inner * middle), middle, inner


class Place:
    def __init__(self, owners):
        self.depth, self.middle, self.inner = grid_of(owners)
        assert self.middle == 2 and self.inner == 2
        self.rep = lax.axis_index("rep")
        me = lax.axis_index("exp")
        x = lax.rem(me, 2)
        y = lax.rem(me // 2, 2)
        self.z = me // 4
        self.me = me
        step_x, step_y = 1 - 2 * x, 2 - 4 * y
        turn = lax.rem(self.rep, 2)
        self.near = (1 - turn) * step_x + turn * step_y
        self.far = turn * step_x + (1 - turn) * step_y
        self.base = me - 4 * self.z

    def line(self, shift, k):
        return self.base + shift + 4 * lax.rem(self.z + k, self.depth)

    def device(self, owner):
        return (self.rep, owner)

    def greet(self, extra=()):
        barrier = pltpu.get_barrier_semaphore()
        partners = [self.device(self.line(0, k)) for k in range(1, self.depth)]
        partners += [self.device(self.me + self.near), self.device(self.me + self.far)]
        partners += list(extra)
        for partner in partners:
            pl.semaphore_signal(barrier, inc=1, device_id=partner, device_id_type=MESH)
        pl.semaphore_wait(barrier, len(partners))


def gather_kernel(owners, x_ref, out_ref, own_sem, send_sem, recv_sem):
    at = Place(owners)
    depth = at.depth
    at.greet()

    def copy(source, owner, slot, target):
        return pltpu.make_async_remote_copy(
            src_ref=source,
            dst_ref=out_ref.at[owner],
            send_sem=send_sem.at[slot],
            recv_sem=recv_sem.at[slot],
            device_id=at.device(target),
            device_id_type=MESH,
        )

    def arrived(owner, slot):
        copy(out_ref.at[owner], owner, slot, at.me).wait_recv()

    near, far = at.me + at.near, at.me + at.far
    line_slot = lambda k: k - 1
    near_slot = lambda k: depth - 1 + k
    far_slot = lambda k: 2 * depth - 1 + k
    turn_slot = lambda k: 3 * depth - 1 + k
    own = pltpu.make_async_copy(x_ref, out_ref.at[at.me], own_sem)
    own.start()
    sent = []

    def send(*what):
        one = copy(*what)
        one.start()
        sent.append(one)

    send(x_ref, at.me, near_slot(0), near)
    send(x_ref, at.me, far_slot(0), far)
    for k in range(1, depth):
        send(x_ref, at.me, line_slot(k), at.line(0, k))
    for k in range(depth):
        back = depth - k
        if k > 0:
            owner = at.line(0, back)
            arrived(owner, line_slot(k))
            send(out_ref.at[owner], owner, near_slot(k), near)
            send(out_ref.at[owner], owner, far_slot(k), far)
        owner = at.line(at.near, back)
        arrived(owner, near_slot(k))
        send(out_ref.at[owner], owner, turn_slot(k), far)
    for k in range(depth):
        arrived(at.line(at.far, depth - k), far_slot(k))
    for k in range(depth):
        arrived(at.line(at.near + at.far, depth - k), turn_slot(k))
    own.wait()
    for one in sent:
        one.wait_send()


def gather_owners(x, owners):
    depth = grid_of(owners)[0]
    copies = 4 * depth - 1
    return pl.pallas_call(
        functools.partial(gather_kernel, owners),
        out_shape=jax.ShapeDtypeStruct((owners,) + x.shape, x.dtype),
        in_specs=[pl.BlockSpec(memory_space=pltpu.VMEM)],
        out_specs=pl.BlockSpec(memory_space=pl.ANY),
        scratch_shapes=[
            pltpu.SemaphoreType.DMA,
            pltpu.SemaphoreType.DMA((copies,)),
            pltpu.SemaphoreType.DMA((copies,)),
        ],
        compiler_params=pltpu.CompilerParams(collective_id=0, has_side_effects=True),
        name="gather_owners",
    )(x)


def scatter_kernel(
    owners, replicas, p_ref, out_ref, rep_in, far_in, near_in, line_in, work, *sems
):
    at = Place(owners)
    depth = at.depth
    (rep_send, rep_recv, far_send, far_recv, near_send, near_recv, line_send, line_recv) = sems
    others = [(lax.rem(at.rep + j, replicas), at.me) for j in range(1, replicas)]
    at.greet(others)
    sent = []

    def copy(source, target, send_sem, recv_sem, device):
        return pltpu.make_async_remote_copy(
            src_ref=source,
            dst_ref=target,
            send_sem=send_sem,
            recv_sem=recv_sem,
            device_id=device,
            device_id_type=MESH,
        )

    lines = [at.near + at.far, at.far, at.near, 0]
    order = [k for k in range(1, depth)] + [0]
    near, far = at.device(at.me + at.near), at.device(at.me + at.far)

    def rep_copy(j, owner):
        return copy(
            p_ref.at[lax.rem(at.rep + j, replicas), owner],
            rep_in.at[j - 1, owner],
            rep_send.at[j - 1, owner],
            rep_recv.at[j - 1, owner],
            (lax.rem(at.rep + j, replicas), at.me),
        )

    for k in range(depth):
        for line in range(4):
            for j in range(1, replicas):
                one = rep_copy(j, at.line(lines[line], order[k]))
                one.start()
                sent.append(one)

    def own(line, k):
        owner = at.line(lines[line], order[k])
        total = p_ref[at.rep if replicas > 1 else 0, owner].astype(jnp.float32)
        for j in range(1, replicas):
            rep_copy(j, owner).wait_recv()
            total = total + rep_in[j - 1, owner].astype(jnp.float32)
        return total

    def far_copy(number):
        return copy(
            work.at[number], far_in.at[number], far_send.at[number], far_recv.at[number], far
        )

    for k in range(depth):
        for line in range(2):
            number = line * depth + k
            work[number] = own(line, k).astype(work.dtype)
            one = far_copy(number)
            one.start()
            sent.append(one)

    def near_copy(k):
        return copy(
            work.at[2 * depth + k], near_in.at[k], near_send.at[k], near_recv.at[k], near
        )

    def near_step(k):
        total = own(2, k)
        far_copy(k).wait_recv()
        work[2 * depth + k] = (total + far_in[k].astype(jnp.float32)).astype(work.dtype)
        one = near_copy(k)
        one.start()
        sent.append(one)

    def line_step(k):
        number = 3 * depth + k
        total = own(3, k)
        far_copy(depth + k).wait_recv()
        near_copy(k).wait_recv()
        total = total + far_in[depth + k].astype(jnp.float32) + near_in[k].astype(jnp.float32)
        if order[k] > 0:
            work[number] = total.astype(work.dtype)
            one = copy(
                work.at[number],
                line_in.at[k],
                line_send.at[k],
                line_recv.at[k],
                at.device(at.line(0, order[k])),
            )
            one.start()
            sent.append(one)
        return total

    for k in range(depth):
        near_step(k)
        if k > 0:
            line_step(k - 1)
    total = line_step(depth - 1)
    for k in range(depth - 1):
        copy(work.at[0], line_in.at[k], line_send.at[k], line_recv.at[k], near).wait_recv()
        total = total + line_in[k].astype(jnp.float32)
    out_ref[...] = total
    for one in sent:
        one.wait_send()


def product_kernel(owners, replicas, left_ref, right_ref, out_ref, p_ref, *rest):
    rows = p_ref.shape[2]
    tile = 2 * rows
    for i in range(replicas * owners // 2):
        part = contract_rows(left_ref[:, i * tile : (i + 1) * tile], right_ref[...])
        part = part.astype(p_ref.dtype)
        for half in range(2):
            p_ref[(2 * i + half) // owners, (2 * i + half) % owners] = part[
                half * rows : (half + 1) * rows
            ]
    scatter_kernel(owners, replicas, p_ref, out_ref, *rest)


def scatter_owners(shape, number, *operands):
    replicas, owners, rows, columns = shape
    kind = jnp.bfloat16
    fused = len(operands) == 2
    p = pltpu.VMEM(shape, kind)
    depth = grid_of(owners)[0]
    dma = pltpu.SemaphoreType.DMA
    many = max(1, replicas - 1)
    rep_slots = owners if replicas > 1 else 1
    return pl.pallas_call(
        functools.partial(product_kernel if fused else scatter_kernel, owners, replicas),
        out_shape=jax.ShapeDtypeStruct((rows, columns), jnp.float32),
        in_specs=[pl.BlockSpec(memory_space=pltpu.VMEM)] * len(operands),
        out_specs=pl.BlockSpec(memory_space=pltpu.VMEM),
        scratch_shapes=[p] * fused
        + [
            pltpu.VMEM((many, rep_slots, rows, columns), kind),
            pltpu.VMEM((2 * depth, rows, columns), kind),
            pltpu.VMEM((depth, rows, columns), kind),
            pltpu.VMEM((depth, rows, columns), kind),
            pltpu.VMEM((4 * depth, rows, columns), kind),
            dma((many, rep_slots)),
            dma((many, rep_slots)),
            dma((2 * depth,)),
            dma((2 * depth,)),
            dma((depth,)),
            dma((depth,)),
            dma((depth,)),
            dma((depth,)),
        ],
        compiler_params=pltpu.CompilerParams(
            collective_id=number, has_side_effects=True, vmem_limit_bytes=60 * 2**20
        ),
        name="scatter_owners",
    )(*operands)


def expert_kernel(
    owners, replicas, x_ref, wg_ref, wu_ref, wd_ref, out_ref, gate_out, up_out, down_out,
    got, work, far_in, near_in, line_in, gate_ref, up_ref, down_ref,
    gate_away, up_away, down_away, gate_came, up_came, down_came, send_sem, recv_sem, *sems
):
    at = Place(owners)
    depth = at.depth
    (far_send, far_recv, near_send, near_recv, line_send, line_recv, rep_send, rep_recv) = sems
    others = [(lax.rem(at.rep + j, replicas), at.me) for j in range(1, replicas)]
    feature = wg_ref.shape[0]
    rows = x_ref.shape[0]
    near, far = at.me + at.near, at.me + at.far
    at.greet(others)
    sent = []

    def copy(source, target, send, recv, owner):
        return pltpu.make_async_remote_copy(
            src_ref=source,
            dst_ref=target,
            send_sem=send,
            recv_sem=recv,
            device_id=at.device(owner),
            device_id_type=MESH,
        )

    def start(one):
        one.start()
        sent.append(one)

    def block_copy(source, owner, slot, target):
        return copy(source, got.at[owner], send_sem.at[slot], recv_sem.at[slot], target)

    def arrived(owner, slot):
        block_copy(got.at[owner], owner, slot, near).wait_recv()

    line_slot = lambda k: k - 1
    near_slot = lambda k: depth - 1 + k
    far_slot = lambda k: 2 * depth - 1 + k
    turn_slot = lambda k: 3 * depth - 1 + k

    def compute(first_block, second_block, first, numbers):
        both = lambda low, high: jnp.concatenate(
            [first_block[:, low:high], second_block[:, low:high]], axis=0
        )
        tail = both(2 * feature, x_ref.shape[1]).astype(jnp.float32)
        lane = lax.broadcasted_iota(jnp.int32, tail.shape, 1)
        mine = (lane == at.me) | (lane == at.me + owners)
        gate = jnp.sum(jnp.where(mine, tail, 0.0), axis=1, keepdims=True)
        rows_in = both(0, feature)
        rows_grad = (both(feature, 2 * feature).astype(jnp.float32) * gate).astype(jnp.bfloat16)
        gate_matrix, up_matrix = wg_ref[...], wu_ref[...]
        pre_gate = jnp.dot(rows_in, gate_matrix, preferred_element_type=jnp.float32)
        pre_up = jnp.dot(rows_in, up_matrix, preferred_element_type=jnp.float32)
        d_hidden = contract_last(rows_grad, wd_ref[...])
        sigma = jax.nn.sigmoid(pre_gate)
        active = pre_gate * sigma
        hidden = (active * pre_up).astype(jnp.bfloat16)
        d_gate = (d_hidden * pre_up * (sigma * (1.0 + pre_gate * (1.0 - sigma)))).astype(
            jnp.bfloat16
        )
        d_up = (d_hidden * active).astype(jnp.bfloat16)
        back = contract_last(d_gate, gate_matrix) + contract_last(d_up, up_matrix)
        back = back.astype(jnp.bfloat16)
        work[numbers[0]] = back[:rows]
        work[numbers[1]] = back[rows:]

        def weights():
            gate_part = contract_rows(rows_in, d_gate)
            up_part = contract_rows(rows_in, d_up)
            down_part = contract_rows(hidden, rows_grad)
            for ref, part in ((gate_ref, gate_part), (up_ref, up_part), (down_ref, down_part)):
                share = ref.shape[2]
                for r in range(replicas):
                    piece = part[:, r * share : (r + 1) * share]
                    if first:
                        ref[r] = piece
                    else:
                        ref[r] += piece

        return weights

    def far_copy(number):
        return copy(
            work.at[number], far_in.at[number], far_send.at[number], far_recv.at[number], far
        )

    def near_copy(k):
        return copy(
            work.at[2 * depth + k], near_in.at[k], near_send.at[k], near_recv.at[k], near
        )

    def line_copy(k, owner):
        return copy(
            work.at[3 * depth + k],
            line_in.at[k - 1],
            line_send.at[k - 1],
            line_recv.at[k - 1],
            owner,
        )

    wide = lambda block: block.astype(jnp.float32)

    def near_step(k):
        number = 2 * depth + k
        far_copy(k).wait_recv()
        work[number] = (wide(work[number]) + wide(far_in[k])).astype(work.dtype)
        start(near_copy(k))

    def line_step(k):
        number = 3 * depth + k
        far_copy(depth + k).wait_recv()
        near_copy(k).wait_recv()
        total = wide(work[number]) + wide(far_in[depth + k]) + wide(near_in[k])
        if k == 0:
            out_ref[...] = total
        else:
            work[number] = total.astype(work.dtype)
            start(line_copy(k, at.line(0, depth - k)))

    start(block_copy(x_ref, at.me, near_slot(0), near))
    start(block_copy(x_ref, at.me, far_slot(0), far))
    for k in range(1, depth):
        start(block_copy(x_ref, at.me, line_slot(k), at.line(0, k)))
    for k in range(depth):
        owner = [at.line(shift, depth - k) for shift in (0, at.near, at.far, at.near + at.far)]
        arrived(owner[1], near_slot(k))
        start(block_copy(got.at[owner[1]], owner[1], turn_slot(k), far))
        if k + 1 < depth:
            later = at.line(0, depth - k - 1)
            arrived(later, line_slot(k + 1))
            start(block_copy(got.at[later], later, near_slot(k + 1), near))
            start(block_copy(got.at[later], later, far_slot(k + 1), far))
        first_block = x_ref if k == 0 else got.at[owner[0]]
        compute(first_block, got.at[owner[1]], k == 0, (3 * depth + k, 2 * depth + k))()
        if k > 0:
            near_step(k - 1)
        arrived(owner[2], far_slot(k))
        arrived(owner[3], turn_slot(k))
        weights = compute(got.at[owner[2]], got.at[owner[3]], False, (depth + k, k))
        start(far_copy(k))
        start(far_copy(depth + k))
        weights()
        if k > 0:
            line_step(k - 1)
    trades = (
        (gate_ref, gate_away, gate_came),
        (up_ref, up_away, up_came),
        (down_ref, down_away, down_came),
    )

    def trade_copy(i, j):
        return pltpu.make_async_remote_copy(
            src_ref=trades[i][1].at[j - 1],
            dst_ref=trades[i][2].at[j - 1],
            send_sem=rep_send.at[i, j - 1],
            recv_sem=rep_recv.at[i, j - 1],
            device_id=others[j - 1],
            device_id_type=MESH,
        )

    for j in range(1, replicas):
        for i in range(3):
            trades[i][1][j - 1] = trades[i][0][lax.rem(at.rep + j, replicas)].astype(jnp.bfloat16)
            start(trade_copy(i, j))
    near_step(depth - 1)
    line_step(depth - 1)
    for i, target in enumerate((gate_out, up_out, down_out)):
        total = trades[i][0][at.rep]
        for j in range(1, replicas):
            trade_copy(i, j).wait_recv()
            total = total + wide(trades[i][2][j - 1])
        target[...] = total
    total = out_ref[...]
    for k in range(1, depth):
        line_copy(k, at.me).wait_recv()
        total = total + wide(line_in[k - 1])
    out_ref[...] = total
    for one in sent:
        one.wait_send()


def expert_on_owners(x, gate_matrix, up_matrix, down_matrix, owners, replicas):
    depth = grid_of(owners)[0]
    rows, columns = x.shape
    feature, hidden = gate_matrix.shape
    dma = pltpu.SemaphoreType.DMA
    copies = 4 * depth - 1
    vmem = pl.BlockSpec(memory_space=pltpu.VMEM)
    block = lambda count: pltpu.VMEM((count, rows, feature), jnp.bfloat16)
    lines = max(1, depth - 1)
    many = max(1, replicas - 1)
    wide = lambda *shape: jax.ShapeDtypeStruct(shape, jnp.float32)
    return pl.pallas_call(
        functools.partial(expert_kernel, owners, replicas),
        out_shape=(
            wide(rows, feature),
            wide(feature, hidden // replicas),
            wide(feature, hidden // replicas),
            wide(hidden, feature // replicas),
        ),
        in_specs=[vmem] * 4,
        out_specs=(vmem,) * 4,
        scratch_shapes=[
            pltpu.VMEM((owners, rows, columns), x.dtype),
            block(4 * depth),
            block(2 * depth),
            block(depth),
            block(lines),
            *(
                pltpu.VMEM((count,) + shape, kind)
                for count, kind in (
                    (replicas, jnp.float32),
                    (many, jnp.bfloat16),
                    (many, jnp.bfloat16),
                )
                for shape in (
                    (feature, hidden // replicas),
                    (feature, hidden // replicas),
                    (hidden, feature // replicas),
                )
            ),
            dma((copies,)),
            dma((copies,)),
            dma((2 * depth,)),
            dma((2 * depth,)),
            dma((depth,)),
            dma((depth,)),
            dma((lines,)),
            dma((lines,)),
            dma((3, many)),
            dma((3, many)),
        ],
        compiler_params=pltpu.CompilerParams(
            collective_id=3, has_side_effects=True, vmem_limit_bytes=60 * 2**20
        ),
        name="expert_on_owners",
    )(x, gate_matrix, up_matrix, down_matrix)


def share_replicas(part, replicas):
    member = lax.axis_index("rep")
    share = part.shape[1] // replicas
    total = lax.dynamic_slice_in_dim(part, member * share, share, 1)
    low = part.astype(jnp.bfloat16)
    for j in range(1, replicas):
        away = lax.dynamic_slice_in_dim(low, lax.rem(member + j, replicas) * share, share, 1)
        came = lax.ppermute(away, "rep", [(i, (i + j) % replicas) for i in range(replicas)])
        total = total + came.astype(jnp.float32)
    return total


def body(attn_out, resid, out_grad, gain, expert_ids, gate_vals, w_gate, w_up, w_down):
    owners = lax.axis_size("exp")
    replicas = lax.axis_size("rep")
    token_rows = expert_ids.shape[0]
    feature = resid.shape[1]
    resid_f = resid.astype(jnp.float32)
    inv_rms = lax.rsqrt(jnp.mean(resid_f * resid_f, axis=1, keepdims=True) + epsilon)
    normed = resid_f * inv_rms
    gain_f = gain[None, :]
    moe_in = (normed * gain_f).astype(jnp.bfloat16)
    hit = expert_ids[:, :, None] == jnp.arange(owners, dtype=jnp.int32)[None, None, :]
    gates = jnp.sum(jnp.where(hit, gate_vals[:, :, None], 0.0), axis=1)
    high = gates.astype(jnp.bfloat16)
    low = (gates - high.astype(jnp.float32)).astype(jnp.bfloat16)
    spare = -(2 * owners) % 128
    sent = jnp.concatenate(
        [moe_in, out_grad, high, low, jnp.zeros((token_rows, spare), jnp.bfloat16)], axis=1
    )
    gate_matrix, up_matrix, down_matrix = w_gate[0], w_up[0], w_down[0]
    held = owners * token_rows * (sent.shape[1] + 2 * feature) * 2
    if held <= 32 * 2**20:
        d_moe, gate_out, up_out, down_out = expert_on_owners(
            sent, gate_matrix, up_matrix, down_matrix, owners, replicas
        )
    else:
        got = gather_owners(sent, owners).reshape(owners * token_rows, sent.shape[1])
        rows_in = got[:, :feature]
        expert = lax.axis_index("exp")
        pick = lambda start: lax.dynamic_slice_in_dim(
            got, start + expert, 1, 1
        ).astype(jnp.float32)
        gate = pick(2 * feature) + pick(2 * feature + owners)
        rows_grad = (got[:, feature : 2 * feature].astype(jnp.float32) * gate).astype(jnp.bfloat16)
        pre_gate = jnp.dot(rows_in, gate_matrix, preferred_element_type=jnp.float32)
        pre_up = jnp.dot(rows_in, up_matrix, preferred_element_type=jnp.float32)
        sigma = jax.nn.sigmoid(pre_gate)
        active = pre_gate * sigma
        hidden = (active * pre_up).astype(jnp.bfloat16)
        d_hidden = contract_last(rows_grad, down_matrix)
        d_gate = (d_hidden * pre_up * (sigma * (1.0 + pre_gate * (1.0 - sigma)))).astype(jnp.bfloat16)
        d_up = (d_hidden * active).astype(jnp.bfloat16)
        back = contract_last(d_gate, gate_matrix) + contract_last(d_up, up_matrix)
        d_moe = scatter_owners(
            (1, owners, token_rows, feature),
            1,
            back.astype(jnp.bfloat16).reshape(1, owners, token_rows, feature),
        )
        gate_part, up_part = contract_rows(rows_in, d_gate), contract_rows(rows_in, d_up)
        down_part = contract_rows(hidden, rows_grad)
        gate_out = share_replicas(gate_part, replicas)
        up_out = share_replicas(up_part, replicas)
        down_out = share_replicas(down_part, replicas)
    d_norm = d_moe * gain_f
    inner = jnp.mean(d_norm * normed, axis=1, keepdims=True)
    d_resid = (out_grad.astype(jnp.float32) + inv_rms * (d_norm - normed * inner)).astype(
        jnp.bfloat16
    )
    rows = attn_out.shape[1] // (owners * replicas)
    shape = (replicas, owners, rows, feature)
    if rows % 64 == 0:
        projection_grad = scatter_owners(shape, 2, attn_out, d_resid)
    else:
        parts = contract_rows(attn_out, d_resid).astype(jnp.bfloat16)
        projection_grad = scatter_owners(shape, 2, parts.reshape(shape))
    return (d_resid, projection_grad, gate_out[None], up_out[None], down_out[None])


def solution(mesh):
    in_specs = (
        P(("rep", "exp"), None),
        P(("rep", "exp"), None),
        P(("rep", "exp"), None),
        P(),
        P(("rep", "exp"), None),
        P(("rep", "exp"), None),
        P("exp", None, None),
        P("exp", None, None),
        P("exp", None, None),
    )
    out_specs = (
        P(("rep", "exp"), None),
        P(("rep", "exp"), None),
        P("exp", None, "rep"),
        P("exp", None, "rep"),
        P("exp", None, "rep"),
    )
    return jax.shard_map(body, mesh=mesh, in_specs=in_specs, out_specs=out_specs, check_vma=False)
```

profile of v0, /device:TPU:0, one launch (start us, length us, event | category | flops | bytes accessed | tf_op | source)
XLA Modules:
  0.0 178.7 jit_solution(7531129740397117532)
XLA Ops:
  0.6 0.0 copy-start
  0.6 0.8 select_reduce_fusion
  1.4 0.1 copy.19
  1.5 0.1 copy.18
  1.6 0.0 copy-done
  1.6 0.0 copy-start.6
  1.7 0.1 fusion.9
  1.8 0.5 copy-done.6
  2.3 0.0 copy-start.5
  2.3 0.1 fusion.3
  2.5 0.1 copy.20
  2.6 0.7 copy-done.5
  3.3 0.9 concatenate.3.x_ref
  4.2 136.3 %expert_on_owners.1 = (f32[128,1024]{1,0:T(8,128)}, f32[1024,256]{1,0:T(8,128)}, f32[1024,256]{1,0:T(8,128)}, f32[512,512]{1,0:T(8,128)}) custom-call(bf16[128,2176]{1,0:T(8,128)(2,1)} %concatenate.3.x_ref, bf16[1024,512]{1,0:T(8,128)(2,1)} %bitcast.6, bf16[1024,512]{1,0:T(8,128)(2,1)} %bitcast.7, bf16[512,1024]{1,0:T(8,128)(2,1)} %bitcast.8), custom_call_target="tpu_custom_call" | custom-call | tf_op jit(solution)/shard_map/expert_on_owners/pallas_call | solution.py:485
  140.5 0.0 copy-start.1
  140.6 1.3 fusion.4
  141.9 0.0 copy-done.1
  141.9 1.0 fusion.8.right_ref
  142.8 0.0 copy-start.4
  142.8 30.0 %scatter_owners.1 = f32[64,1024]{1,0:T(8,128)} custom-call(bf16[128,2048]{1,0:T(8,128)(2,1)} %left_ref.1, bf16[128,1024]{1,0:T(8,128)(2,1)} %fusion.8.right_ref), custom_call_target="tpu_custom_call" | custom-call | tf_op jit(solution)/shard_map/scatter_owners/pallas_call | solution.py:265
  172.9 1.7 copy.25
  174.5 0.0 copy-done.4
  174.6 0.0 copy-start.3
  174.6 1.0 copy.26
  175.5 0.6 copy-done.3
  176.2 0.0 copy-start.2
  176.2 1.0 copy.27
  177.1 0.6 copy-done.2
  177.8 1.0 copy.28
  (5 shorter events, 0.0 us)
Async XLA Ops:
  0.6 1.0 copy-start
  1.6 0.7 copy-start.6
  2.3 0.9 copy-start.5
  140.5 1.3 copy-start.1
  142.8 31.7 %copy-start.4 = (f32[1024,256]{1,0:T(8,128)S(1)}, f32[1024,256]{1,0:T(8,128)}, u32[]{:S(2)}) copy-start(f32[1024,256]{1,0:T(8,128)} %get-tuple-element.10) | copy-start | bytes 3145732
  174.6 1.6 copy-start.3
  176.2 1.6 copy-start.2
where the time goes:
time: 179 us
  Pallas kernels  166 us (93%)
  local copies, waits for them, and re-layouts  8.36 us (5%)
  other arithmetic  3.33 us (2%)
    pallas_call x1, Pallas kernels, expert_on_owners(): pl.pallas_call(functools.partial(expert_kernel, owners, replicas), out_sh...  136 us
    pallas_call x1, Pallas kernels, scatter_owners(): pl.pallas_call(functools.partial(product_kernel if fused else scatter_ker...  30 us
    unnamed x18, local copies, waits for them, and re-layouts  7.08 us

commit v1 on v0

--- a/solution.py
+++ b/solution.py
@@ -9,6 +9,7 @@
 
 epsilon = 1e-06
 MESH = pl.DeviceIdType.MESH
+NEAR_BY_LINE = (True, False, False)
 
 
 def contract_rows(left, right):
@@ -290,18 +291,55 @@
     )(*operands)
 
 
+def steps_of(depth, z):
+    side = jnp.minimum(z, depth - 1 - z)
+    planes = [z]
+    for k in range(1, depth):
+        turn = z - (k + 1) // 2 if k % 2 else z + k // 2
+        rest = jnp.where(z > depth - 1 - z, z - (k - side), z + (k - side))
+        planes.append(jnp.where(k <= 2 * side, turn, rest))
+    return planes
+
+
 def expert_kernel(
-    owners, replicas, x_ref, wg_ref, wu_ref, wd_ref, out_ref, gate_out, up_out, down_out,
-    got, work, far_in, near_in, line_in, gate_ref, up_ref, down_ref,
-    gate_away, up_away, down_away, gate_came, up_came, down_came, send_sem, recv_sem, *sems
+    owners, replicas, cap, near_by_line, resid_ref, grad_ref, gain_ref, ids_ref, vals_ref,
+    gate_hbm, up_hbm, down_hbm, out_ref, gate_out, up_out, down_out,
+    wide_ref, deep_ref, got_x, got_g, got_t, pick_ref, all_x, all_g, all_d, all_h,
+    leaf_x, leaf_g, ret, leaf_back, root_sum, near_work, near_in, line_work, line_in,
+    first_ref, second_ref, gate_away, up_away, down_away, gate_came, up_came, down_came,
+    load_sem, own_send, hop_send, line_recv, side_send, side_recv, leaf_send, leaf_recv,
+    back_send, back_recv, near_send, near_recv, home_send, home_recv, rep_send, rep_recv,
 ):
     at = Place(owners)
-    depth = at.depth
-    (far_send, far_recv, near_send, near_recv, line_send, line_recv, rep_send, rep_recv) = sems
+    depth, z = at.depth, at.z
+    rows, feature = resid_ref.shape
+    hidden = deep_ref.shape[0]
+    pair = 2 * cap
     others = [(lax.rem(at.rep + j, replicas), at.me) for j in range(1, replicas)]
-    feature = wg_ref.shape[0]
-    rows = x_ref.shape[0]
+    planes = steps_of(depth, z)
+    wide = lambda block: block.astype(jnp.float32)
     near, far = at.me + at.near, at.me + at.far
+    owner_at = lambda plane: at.base + 4 * plane
+
+    loads = [
+        pltpu.make_async_copy(gate_hbm, wide_ref.at[:, pl.ds(0, hidden)], load_sem.at[0]),
+        pltpu.make_async_copy(up_hbm, wide_ref.at[:, pl.ds(hidden, hidden)], load_sem.at[1]),
+        pltpu.make_async_copy(down_hbm, deep_ref, load_sem.at[2]),
+    ]
+    for one in loads:
+        one.start()
+
+    resid = wide(resid_ref[...])
+    inv_rms = lax.rsqrt(jnp.mean(resid * resid, axis=1, keepdims=True) + epsilon)
+    normed = resid * inv_rms
+    got_x[z, pl.ds(0, rows)] = (normed * gain_ref[...]).astype(jnp.bfloat16)
+    got_g[z, pl.ds(0, rows)] = grad_ref[...]
+    number = lax.broadcasted_iota(jnp.int32, (owners, rows), 0)
+    table = jnp.zeros((owners, rows), jnp.float32)
+    for j in range(ids_ref.shape[0]):
+        table = table + jnp.where(ids_ref[j : j + 1, :] == number, vals_ref[j : j + 1, :], 0.0)
+    got_t[z, pl.ds(0, owners)] = table
+
     at.greet(others)
     sent = []
 
@@ -317,133 +355,221 @@
 
     def start(one):
         one.start()
-        sent.append(one)
-
-    def block_copy(source, owner, slot, target):
-        return copy(source, got.at[owner], send_sem.at[slot], recv_sem.at[slot], target)
-
-    def arrived(owner, slot):
-        block_copy(got.at[owner], owner, slot, near).wait_recv()
-
-    line_slot = lambda k: k - 1
-    near_slot = lambda k: depth - 1 + k
-    far_slot = lambda k: 2 * depth - 1 + k
-    turn_slot = lambda k: 3 * depth - 1 + k
-
-    def compute(first_block, second_block, first, numbers):
-        both = lambda low, high: jnp.concatenate(
-            [first_block[:, low:high], second_block[:, low:high]], axis=0
-        )
-        tail = both(2 * feature, x_ref.shape[1]).astype(jnp.float32)
-        lane = lax.broadcasted_iota(jnp.int32, tail.shape, 1)
-        mine = (lane == at.me) | (lane == at.me + owners)
-        gate = jnp.sum(jnp.where(mine, tail, 0.0), axis=1, keepdims=True)
-        rows_in = both(0, feature)
-        rows_grad = (both(feature, 2 * feature).astype(jnp.float32) * gate).astype(jnp.bfloat16)
-        gate_matrix, up_matrix = wg_ref[...], wu_ref[...]
-        pre_gate = jnp.dot(rows_in, gate_matrix, preferred_element_type=jnp.float32)
-        pre_up = jnp.dot(rows_in, up_matrix, preferred_element_type=jnp.float32)
-        d_hidden = contract_last(rows_grad, wd_ref[...])
+        sent.append((None, one))
+
+    def start_if(ok, one):
+        @pl.when(ok)
+        def _():
+            one.start()
+
+        sent.append((ok, one))
+
+    def piece(name, role, plane):
+        if name == 2:
+            return got_t.at[plane, pl.ds(role * owners, owners)]
+        return (got_x, got_g)[name].at[plane, pl.ds(role * rows, rows)]
+
+    def own_hops(role, name):
+        for way in range(2):
+            target = z + 1 - 2 * way
+            block = piece(name, role, z)
+            start_if(
+                (target >= 0) & (target < depth),
+                copy(
+                    block, block, own_send.at[role, name, way], line_recv.at[role, name, z],
+                    owner_at(target),
+                ),
+            )
+
+    def hop(role, name, k):
+        plane = planes[k]
+        block = piece(name, role, plane)
+        target = jnp.where(plane < z, z + 1, z - 1)
+        one = copy(
+            block, block, hop_send.at[role, name, k], line_recv.at[role, name, plane],
+            owner_at(target),
+        )
+        one.wait_recv()
+        start_if((target >= 0) & (target < depth), one)
+
+    def side(name, k):
+        return copy(
+            piece(name, 0, planes[k]), piece(name, 1, planes[k]),
+            side_send.at[name, k], side_recv.at[name, k], near,
+        )
+
+    by_line = lambda name, k: k > 0 and near_by_line[name]
+
+    def relay(k, names):
+        for name in names:
+            if k == 0:
+                own_hops(0, name)
+            else:
+                hop(0, name, k)
+            if not by_line(name, k):
+                start(side(name, k))
+
+    def near_ready(k, names):
+        for name in names:
+            if by_line(name, k):
+                hop(1, name, k)
+            else:
+                side(name, k).wait_recv()
+                if k == 0 and near_by_line[name]:
+                    own_hops(1, name)
+
+    def leaf(name, k):
+        target = (all_x, all_g)[name].at[pl.ds((2 * k + 1) * pair, pair)]
+        source = (leaf_x, leaf_g)[name].at[k]
+        return copy(source, target, leaf_send.at[name, k], leaf_recv.at[name, k], far)
+
+    def select(k):
+        plane = planes[k]
+        near_ready(k, (2,))
+        gates = got_t[plane]
+        hit = gates > 0.0
+        lower = lax.broadcasted_iota(jnp.int32, (rows, rows), 0)
+        upper = lax.broadcasted_iota(jnp.int32, (rows, rows), 1)
+        ramp = jnp.where(lower <= upper, 1.0, 0.0).astype(jnp.bfloat16)
+        place = jnp.dot(
+            jnp.where(hit, 1.0, 0.0).astype(jnp.bfloat16), ramp, preferred_element_type=jnp.float32
+        )
+        place = jnp.where(hit, place, 0.0)
+        line = lax.broadcasted_iota(jnp.int32, gates.shape, 0)
+        order = (lax.broadcasted_iota(jnp.int32, (cap, rows), 0) + 1).astype(jnp.float32)
+        empty = jnp.zeros((cap, rows), jnp.float32)
+        picks, weights = [], []
+        for expert in (at.me, far):
+            for role in range(2):
+                mine = line == expert + role * owners
+                spot = jnp.sum(jnp.where(mine, place, 0.0), axis=0, keepdims=True)
+                value = jnp.sum(jnp.where(mine, gates, 0.0), axis=0, keepdims=True)
+                one_hot = jnp.where(order == spot, 1.0, 0.0)
+                weights.append(jnp.sum(one_hot * value, axis=1, keepdims=True))
+                picks.append(
+                    jnp.concatenate([one_hot, empty] if role == 0 else [empty, one_hot], axis=1)
+                )
+        pick = jnp.concatenate(picks, axis=0).astype(jnp.bfloat16)
+        weight = jnp.concatenate(weights, axis=0)
+        pick_ref[k] = pick
+        low = 2 * k * pair
+        near_ready(k, (0,))
+        chosen = jnp.dot(pick, got_x[plane], preferred_element_type=jnp.float32)
+        chosen = chosen.astype(jnp.bfloat16)
+        leaf_x[k] = chosen[pair:]
+        start(leaf(0, k))
+        all_x[low : low + pair] = chosen[:pair]
+        near_ready(k, (1,))
+        chosen = jnp.dot(pick, got_g[plane], preferred_element_type=jnp.float32) * weight
+        chosen = chosen.astype(jnp.bfloat16)
+        leaf_g[k] = chosen[pair:]
+        start(leaf(1, k))
+        all_g[low : low + pair] = chosen[:pair]
+
+    def compute(k, half):
+        low = (2 * k + half) * pair
+        rows_in, rows_grad = all_x[low : low + pair], all_g[low : low + pair]
+        matrix = wide_ref[...]
+        pre = jnp.dot(rows_in, matrix, preferred_element_type=jnp.float32)
+        d_hidden = contract_last(rows_grad, deep_ref[...])
+        pre_gate, pre_up = pre[:, :hidden], pre[:, hidden:]
         sigma = jax.nn.sigmoid(pre_gate)
         active = pre_gate * sigma
-        hidden = (active * pre_up).astype(jnp.bfloat16)
+        all_h[low : low + pair] = (active * pre_up).astype(jnp.bfloat16)
         d_gate = (d_hidden * pre_up * (sigma * (1.0 + pre_gate * (1.0 - sigma)))).astype(
             jnp.bfloat16
         )
         d_up = (d_hidden * active).astype(jnp.bfloat16)
-        back = contract_last(d_gate, gate_matrix) + contract_last(d_up, up_matrix)
-        back = back.astype(jnp.bfloat16)
-        work[numbers[0]] = back[:rows]
-        work[numbers[1]] = back[rows:]
-
-        def weights():
-            gate_part = contract_rows(rows_in, d_gate)
-            up_part = contract_rows(rows_in, d_up)
-            down_part = contract_rows(hidden, rows_grad)
-            for ref, part in ((gate_ref, gate_part), (up_ref, up_part), (down_ref, down_part)):
-                share = ref.shape[2]
-                for r in range(replicas):
-                    piece = part[:, r * share : (r + 1) * share]
-                    if first:
-                        ref[r] = piece
-                    else:
-                        ref[r] += piece
-
-        return weights
-
-    def far_copy(number):
+        all_d[low : low + pair, :hidden] = d_gate
+        all_d[low : low + pair, hidden:] = d_up
+        back = contract_last(jnp.concatenate([d_gate, d_up], axis=1), matrix).astype(jnp.bfloat16)
+        if half == 0:
+            ret[k, :pair] = back
+        else:
+            leaf_back[k] = back
+            start(back_copy(k))
+
+    def back_copy(k):
         return copy(
-            work.at[number], far_in.at[number], far_send.at[number], far_recv.at[number], far
+            leaf_back.at[k], ret.at[k, pl.ds(pair, pair)], back_send.at[k], back_recv.at[k], far
         )
 
     def near_copy(k):
+        return copy(near_work.at[k], near_in.at[k], near_send.at[k], near_recv.at[k], near)
+
+    def home_copy(k, plane, slot):
         return copy(
-            work.at[2 * depth + k], near_in.at[k], near_send.at[k], near_recv.at[k], near
-        )
-
-    def line_copy(k, owner):
-        return copy(
-            work.at[3 * depth + k],
-            line_in.at[k - 1],
-            line_send.at[k - 1],
-            line_recv.at[k - 1],
-            owner,
-        )
-
-    wide = lambda block: block.astype(jnp.float32)
+            line_work.at[k], line_in.at[slot], home_send.at[k], home_recv.at[slot], owner_at(plane)
+        )
+
+    def leaf_step(k):
+        leaf(0, k).wait_recv()
+        leaf(1, k).wait_recv()
+        compute(k, 1)
 
     def near_step(k):
-        number = 2 * depth + k
-        far_copy(k).wait_recv()
-        work[number] = (wide(work[number]) + wide(far_in[k])).astype(work.dtype)
+        back_copy(k).wait_recv()
+        total = contract_rows(pick_ref[k], ret[k])
+        near_work[k] = total[rows:].astype(jnp.bfloat16)
         start(near_copy(k))
-
-    def line_step(k):
-        number = 3 * depth + k
-        far_copy(depth + k).wait_recv()
+        root_sum[k] = total[:rows]
+
+    def root_step(k):
         near_copy(k).wait_recv()
-        total = wide(work[number]) + wide(far_in[depth + k]) + wide(near_in[k])
+        total = root_sum[k] + wide(near_in[k])
         if k == 0:
-            out_ref[...] = total
+            root_sum[k] = total
         else:
-            work[number] = total.astype(work.dtype)
-            start(line_copy(k, at.line(0, depth - k)))
-
-    start(block_copy(x_ref, at.me, near_slot(0), near))
-    start(block_copy(x_ref, at.me, far_slot(0), far))
-    for k in range(1, depth):
-        start(block_copy(x_ref, at.me, line_slot(k), at.line(0, k)))
+            line_work[k] = total.astype(jnp.bfloat16)
+            start(home_copy(k, planes[k], z))
+
+    def weights(first, last):
+        low, high = 2 * first * pair, 2 * last * pair
+        wide_part = contract_rows(all_x[low:high], all_d[low:high])
+        deep_part = contract_rows(all_h[low:high], all_g[low:high])
+        if first == 0:
+            first_ref[...] = wide_part
+            second_ref[...] = deep_part
+        else:
+            first_ref[...] += wide_part
+            second_ref[...] += deep_part
+
+    relay(0, (2, 0, 1))
+    select(0)
+    for one in loads:
+        one.wait()
     for k in range(depth):
-        owner = [at.line(shift, depth - k) for shift in (0, at.near, at.far, at.near + at.far)]
-        arrived(owner[1], near_slot(k))
-        start(block_copy(got.at[owner[1]], owner[1], turn_slot(k), far))
         if k + 1 < depth:
-            later = at.line(0, depth - k - 1)
-            arrived(later, line_slot(k + 1))
-            start(block_copy(got.at[later], later, near_slot(k + 1), near))
-            start(block_copy(got.at[later], later, far_slot(k + 1), far))
-        first_block = x_ref if k == 0 else got.at[owner[0]]
-        compute(first_block, got.at[owner[1]], k == 0, (3 * depth + k, 2 * depth + k))()
+            relay(k + 1, (2, 0))
+        compute(k, 0)
+        if k + 1 < depth:
+            relay(k + 1, (1,))
         if k > 0:
             near_step(k - 1)
-        arrived(owner[2], far_slot(k))
-        arrived(owner[3], turn_slot(k))
-        weights = compute(got.at[owner[2]], got.at[owner[3]], False, (depth + k, k))
-        start(far_copy(k))
-        start(far_copy(depth + k))
-        weights()
+        leaf_step(k)
+        if k + 1 < depth:
+            select(k + 1)
         if k > 0:
-            line_step(k - 1)
+            root_step(k - 1)
+        if k == depth // 2:
+            weights(0, depth // 2)
+    weights(depth // 2, depth)
+
+    share, deep_share = hidden // replicas, feature // replicas
     trades = (
-        (gate_ref, gate_away, gate_came),
-        (up_ref, up_away, up_came),
-        (down_ref, down_away, down_came),
+        (first_ref, 0, share, gate_away, gate_came, gate_out),
+        (first_ref, hidden, share, up_away, up_came, up_out),
+        (second_ref, 0, deep_share, down_away, down_came, down_out),
     )
+
+    def part_of(i, member):
+        ref, low, size = trades[i][:3]
+        return ref[:, pl.ds(pl.multiple_of(low + member * size, 128), size)]
 
     def trade_copy(i, j):
         return pltpu.make_async_remote_copy(
-            src_ref=trades[i][1].at[j - 1],
-            dst_ref=trades[i][2].at[j - 1],
+            src_ref=trades[i][3].at[j - 1],
+            dst_ref=trades[i][4].at[j - 1],
             send_sem=rep_send.at[i, j - 1],
             recv_sem=rep_recv.at[i, j - 1],
             device_id=others[j - 1],
@@ -452,73 +578,96 @@
 
     for j in range(1, replicas):
         for i in range(3):
-            trades[i][1][j - 1] = trades[i][0][lax.rem(at.rep + j, replicas)].astype(jnp.bfloat16)
+            trades[i][3][j - 1] = part_of(i, lax.rem(at.rep + j, replicas)).astype(jnp.bfloat16)
             start(trade_copy(i, j))
     near_step(depth - 1)
-    line_step(depth - 1)
-    for i, target in enumerate((gate_out, up_out, down_out)):
-        total = trades[i][0][at.rep]
+    for i in range(3):
+        total = part_of(i, at.rep)
         for j in range(1, replicas):
             trade_copy(i, j).wait_recv()
-            total = total + wide(trades[i][2][j - 1])
-        target[...] = total
-    total = out_ref[...]
+            total = total + wide(trades[i][4][j - 1])
+        trades[i][5][...] = total
+    root_step(depth - 1)
+    d_moe = root_sum[0]
     for k in range(1, depth):
-        line_copy(k, at.me).wait_recv()
-        total = total + wide(line_in[k - 1])
-    out_ref[...] = total
-    for one in sent:
-        one.wait_send()
-
-
-def expert_on_owners(x, gate_matrix, up_matrix, down_matrix, owners, replicas):
+        home_copy(k, z, planes[k]).wait_recv()
+        d_moe = d_moe + wide(line_in[planes[k]])
+    d_norm = d_moe * gain_ref[...]
+    resid = wide(resid_ref[...])
+    inv_rms = lax.rsqrt(jnp.mean(resid * resid, axis=1, keepdims=True) + epsilon)
+    normed = resid * inv_rms
+    inner = jnp.mean(d_norm * normed, axis=1, keepdims=True)
+    out_ref[...] = (wide(grad_ref[...]) + inv_rms * (d_norm - normed * inner)).astype(jnp.bfloat16)
+    for ok, one in sent:
+        if ok is None:
+            one.wait_send()
+        else:
+            pl.when(ok)(one.wait_send)
+
+
+def expert_on_owners(
+    resid, out_grad, gain, ids, vals, gate_matrix, up_matrix, down_matrix, cap, owners, replicas
+):
     depth = grid_of(owners)[0]
-    rows, columns = x.shape
-    feature, hidden = gate_matrix.shape
+    rows, feature = resid.shape
+    hidden = gate_matrix.shape[1]
     dma = pltpu.SemaphoreType.DMA
-    copies = 4 * depth - 1
+    pair = 2 * cap
     vmem = pl.BlockSpec(memory_space=pltpu.VMEM)
-    block = lambda count: pltpu.VMEM((count, rows, feature), jnp.bfloat16)
-    lines = max(1, depth - 1)
+    hbm = pl.BlockSpec(memory_space=pl.ANY)
+    low = lambda *shape: pltpu.VMEM(shape, jnp.bfloat16)
+    high = lambda *shape: pltpu.VMEM(shape, jnp.float32)
     many = max(1, replicas - 1)
     wide = lambda *shape: jax.ShapeDtypeStruct(shape, jnp.float32)
+    shares = [
+        (feature, hidden // replicas),
+        (feature, hidden // replicas),
+        (hidden, feature // replicas),
+    ]
     return pl.pallas_call(
-        functools.partial(expert_kernel, owners, replicas),
-        out_shape=(
-            wide(rows, feature),
-            wide(feature, hidden // replicas),
-            wide(feature, hidden // replicas),
-            wide(hidden, feature // replicas),
-        ),
-        in_specs=[vmem] * 4,
+        functools.partial(expert_kernel, owners, replicas, cap, NEAR_BY_LINE),
+        out_shape=(jax.ShapeDtypeStruct((rows, feature), jnp.bfloat16),)
+        + tuple(wide(*shape) for shape in shares),
+        in_specs=[vmem] * 5 + [hbm] * 3,
         out_specs=(vmem,) * 4,
         scratch_shapes=[
-            pltpu.VMEM((owners, rows, columns), x.dtype),
-            block(4 * depth),
-            block(2 * depth),
-            block(depth),
-            block(lines),
-            *(
-                pltpu.VMEM((count,) + shape, kind)
-                for count, kind in (
-                    (replicas, jnp.float32),
-                    (many, jnp.bfloat16),
-                    (many, jnp.bfloat16),
-                )
-                for shape in (
-                    (feature, hidden // replicas),
-                    (feature, hidden // replicas),
-                    (hidden, feature // replicas),
-                )
-            ),
-            dma((copies,)),
-            dma((copies,)),
-            dma((2 * depth,)),
-            dma((2 * depth,)),
-            dma((depth,)),
-            dma((depth,)),
-            dma((lines,)),
-            dma((lines,)),
+            low(feature, 2 * hidden),
+            low(hidden, feature),
+            low(depth, 2 * rows, feature),
+            low(depth, 2 * rows, feature),
+            high(depth, 2 * owners, rows),
+            low(depth, 2 * pair, 2 * rows),
+            low(depth * 2 * pair, feature),
+            low(depth * 2 * pair, feature),
+            low(depth * 2 * pair, 2 * hidden),
+            low(depth * 2 * pair, hidden),
+            low(depth, pair, feature),
+            low(depth, pair, feature),
+            low(depth, 2 * pair, feature),
+            low(depth, pair, feature),
+            high(depth, rows, feature),
+            low(depth, rows, feature),
+            low(depth, rows, feature),
+            low(depth, rows, feature),
+            low(depth, rows, feature),
+            high(feature, 2 * hidden),
+            high(hidden, feature),
+            *(low(many, *shape) for shape in shares),
+            *(low(many, *shape) for shape in shares),
+            dma((3,)),
+            dma((2, 3, 2)),
+            dma((2, 3, depth)),
+            dma((2, 3, depth)),
+            dma((3, depth)),
+            dma((3, depth)),
+            dma((2, depth)),
+            dma((2, depth)),
+            dma((depth,)),
+            dma((depth,)),
+            dma((depth,)),
+            dma((depth,)),
+            dma((depth,)),
+            dma((depth,)),
             dma((3, many)),
             dma((3, many)),
         ],
@@ -526,7 +675,7 @@
             collective_id=3, has_side_effects=True, vmem_limit_bytes=60 * 2**20
         ),
         name="expert_on_owners",
-    )(x, gate_matrix, up_matrix, down_matrix)
+    )(resid, out_grad, gain, ids, vals, gate_matrix, up_matrix, down_matrix)
 
 
 def share_replicas(part, replicas):
@@ -544,12 +693,41 @@
 def body(attn_out, resid, out_grad, gain, expert_ids, gate_vals, w_gate, w_up, w_down):
     owners = lax.axis_size("exp")
     replicas = lax.axis_size("rep")
+    token_rows, top = expert_ids.shape
+    feature = resid.shape[1]
+    gain_f = gain[None, :]
+    gate_matrix, up_matrix, down_matrix = w_gate[0], w_up[0], w_down[0]
+    cap = 9 * token_rows * top // (8 * owners)
+    held = owners * token_rows * 4 * feature * 2
+    if held <= 32 * 2**20:
+        d_resid, gate_out, up_out, down_out = expert_on_owners(
+            resid, out_grad, gain_f, expert_ids.T, gate_vals.T, gate_matrix, up_matrix,
+            down_matrix, cap, owners, replicas
+        )
+    else:
+        d_resid, gate_out, up_out, down_out = experts_by_gather(
+            resid, out_grad, gain_f, expert_ids, gate_vals, gate_matrix, up_matrix, down_matrix
+        )
+    rows = attn_out.shape[1] // (owners * replicas)
+    shape = (replicas, owners, rows, feature)
+    if rows % 64 == 0:
+        projection_grad = scatter_owners(shape, 2, attn_out, d_resid)
+    else:
+        parts = contract_rows(attn_out, d_resid).astype(jnp.bfloat16)
+        projection_grad = scatter_owners(shape, 2, parts.reshape(shape))
+    return (d_resid, projection_grad, gate_out[None], up_out[None], down_out[None])
+
+
+def experts_by_gather(
+    resid, out_grad, gain_f, expert_ids, gate_vals, gate_matrix, up_matrix, down_matrix
+):
+    owners = lax.axis_size("exp")
+    replicas = lax.axis_size("rep")
     token_rows = expert_ids.shape[0]
     feature = resid.shape[1]
     resid_f = resid.astype(jnp.float32)
     inv_rms = lax.rsqrt(jnp.mean(resid_f * resid_f, axis=1, keepdims=True) + epsilon)
     normed = resid_f * inv_rms
-    gain_f = gain[None, :]
     moe_in = (normed * gain_f).astype(jnp.bfloat16)
     hit = expert_ids[:, :, None] == jnp.arange(owners, dtype=jnp.int32)[None, None, :]
     gates = jnp.sum(jnp.where(hit, gate_vals[:, :, None], 0.0), axis=1)
@@ -559,53 +737,39 @@
     sent = jnp.concatenate(
         [moe_in, out_grad, high, low, jnp.zeros((token_rows, spare), jnp.bfloat16)], axis=1
     )
-    gate_matrix, up_matrix, down_matrix = w_gate[0], w_up[0], w_down[0]
-    held = owners * token_rows * (sent.shape[1] + 2 * feature) * 2
-    if held <= 32 * 2**20:
-        d_moe, gate_out, up_out, down_out = expert_on_owners(
-            sent, gate_matrix, up_matrix, down_matrix, owners, replicas
-        )
-    else:
-        got = gather_owners(sent, owners).reshape(owners * token_rows, sent.shape[1])
-        rows_in = got[:, :feature]
-        expert = lax.axis_index("exp")
-        pick = lambda start: lax.dynamic_slice_in_dim(
-            got, start + expert, 1, 1
-        ).astype(jnp.float32)
-        gate = pick(2 * feature) + pick(2 * feature + owners)
-        rows_grad = (got[:, feature : 2 * feature].astype(jnp.float32) * gate).astype(jnp.bfloat16)
-        pre_gate = jnp.dot(rows_in, gate_matrix, preferred_element_type=jnp.float32)
-        pre_up = jnp.dot(rows_in, up_matrix, preferred_element_type=jnp.float32)
-        sigma = jax.nn.sigmoid(pre_gate)
-        active = pre_gate * sigma
-        hidden = (active * pre_up).astype(jnp.bfloat16)
-        d_hidden = contract_last(rows_grad, down_matrix)
-        d_gate = (d_hidden * pre_up * (sigma * (1.0 + pre_gate * (1.0 - sigma)))).astype(jnp.bfloat16)
-        d_up = (d_hidden * active).astype(jnp.bfloat16)
-        back = contract_last(d_gate, gate_matrix) + contract_last(d_up, up_matrix)
-        d_moe = scatter_owners(
-            (1, owners, token_rows, feature),
-            1,
-            back.astype(jnp.bfloat16).reshape(1, owners, token_rows, feature),
-        )
-        gate_part, up_part = contract_rows(rows_in, d_gate), contract_rows(rows_in, d_up)
-        down_part = contract_rows(hidden, rows_grad)
-        gate_out = share_replicas(gate_part, replicas)
-        up_out = share_replicas(up_part, replicas)
-        down_out = share_replicas(down_part, replicas)
+    got = gather_owners(sent, owners).reshape(owners * token_rows, sent.shape[1])
+    rows_in = got[:, :feature]
+    expert = lax.axis_index("exp")
+    pick = lambda start: lax.dynamic_slice_in_dim(
+        got, start + expert, 1, 1
+    ).astype(jnp.float32)
+    gate = pick(2 * feature) + pick(2 * feature + owners)
+    rows_grad = (got[:, feature : 2 * feature].astype(jnp.float32) * gate).astype(jnp.bfloat16)
+    pre_gate = jnp.dot(rows_in, gate_matrix, preferred_element_type=jnp.float32)
+    pre_up = jnp.dot(rows_in, up_matrix, preferred_element_type=jnp.float32)
+    sigma = jax.nn.sigmoid(pre_gate)
+    active = pre_gate * sigma
+    hidden = (active * pre_up).astype(jnp.bfloat16)
+    d_hidden = contract_last(rows_grad, down_matrix)
+    d_gate = (d_hidden * pre_up * (sigma * (1.0 + pre_gate * (1.0 - sigma)))).astype(jnp.bfloat16)
+    d_up = (d_hidden * active).astype(jnp.bfloat16)
+    back = contract_last(d_gate, gate_matrix) + contract_last(d_up, up_matrix)
+    d_moe = scatter_owners(
+        (1, owners, token_rows, feature),
+        1,
+        back.astype(jnp.bfloat16).reshape(1, owners, token_rows, feature),
+    )
+    gate_part, up_part = contract_rows(rows_in, d_gate), contract_rows(rows_in, d_up)
+    down_part = contract_rows(hidden, rows_grad)
+    gate_out = share_replicas(gate_part, replicas)
+    up_out = share_replicas(up_part, replicas)
+    down_out = share_replicas(down_part, replicas)
     d_norm = d_moe * gain_f
     inner = jnp.mean(d_norm * normed, axis=1, keepdims=True)
     d_resid = (out_grad.astype(jnp.float32) + inv_rms * (d_norm - normed * inner)).astype(
         jnp.bfloat16
     )
-    rows = attn_out.shape[1] // (owners * replicas)
-    shape = (replicas, owners, rows, feature)
-    if rows % 64 == 0:
-        projection_grad = scatter_owners(shape, 2, attn_out, d_resid)
-    else:
-        parts = contract_rows(attn_out, d_resid).astype(jnp.bfloat16)
-        projection_grad = scatter_owners(shape, 2, parts.reshape(shape))
-    return (d_resid, projection_grad, gate_out[None], up_out[None], down_out[None])
+    return d_resid, gate_out, up_out, down_out
 
 
 def solution(mesh):

time: 179 us -> 143 us (0.80)
  Pallas kernels: 166 us -> 136 us
  other arithmetic: 3.33 us -> 0 us
  local copies, waits for them, and re-layouts: 8.36 us -> 5.92 us
    pallas_call x1, Pallas kernels: 136 us -> 103 us  [expert_on_owners(): pl.pallas_call(functools.partial(expert_kernel, owners, replicas, cap, NE...]
    pallas_call x1, Pallas kernels: 30 us -> 32.7 us  [scatter_owners(): pl.pallas_call(functools.partial(product_kernel if fused else scatter_ker...]
    reduce_sum x3 -> x0, other arithmetic: 2.22 us -> none  [the longest x1 1.32 us: body(): inner = jnp.mean(d_norm * normed, axis=1, keepdims=True)]
    unnamed x18 -> x15, local copies, waits for them, and re-layouts: 7.08 us -> 5.92 us
where the time goes in v1:
time: 143 us; the launch traced here: 142 us
  Pallas kernels  136 us (95%)
  local copies, waits for them, and re-layouts  5.92 us (4%)
    pallas_call x1, Pallas kernels, expert_on_owners(): pl.pallas_call(functools.partial(expert_kernel, owners, replicas, cap, NE...  103 us
    pallas_call x1, Pallas kernels, scatter_owners(): pl.pallas_call(functools.partial(product_kernel if fused else scatter_ker...  32.7 us
    unnamed x15, local copies, waits for them, and re-layouts  5.92 us

profile of v1, /device:TPU:0, one launch (start us, length us, event | category | flops | bytes accessed | tf_op | source)
XLA Modules:
  0.0 142.5 jit_solution(10059908821054106840)
XLA Ops:
  0.6 103.2 %expert_on_owners.1 = (bf16[128,1024]{1,0:T(8,128)(2,1)}, f32[1024,256]{1,0:T(8,128)}, f32[1024,256]{1,0:T(8,128)}, f32[512,512]{1,0:T(8,128)}) custom-call(bf16[128,1024]{1,0:T(8,128)(2,1)} %resid_ref.1, bf16[128,1024]{1,0:T(8,128)(2,1)} %grad_ref.1, f32[1,1024]{1,0:T(1,128)} %bitcast.15, s32[8,128]{1,0:T(8,128)} %bitcast.16, f32[8,128]{1,0:T(8,128)} %bitcast.17, ...), custom_call_target="tpu_custom_call" | custom-call | tf_op jit(solution)/shard_map/expert_on_owners/pallas_call | solution.py:627
  103.8 0.0 copy-start.3
  103.8 0.0 copy-start.2
  103.9 32.7 %scatter_owners.1 = f32[64,1024]{1,0:T(8,128)} custom-call(bf16[128,2048]{1,0:T(8,128)(2,1)} %left_ref.1, bf16[128,1024]{1,0:T(8,128)(2,1)} %get-tuple-element.18.right_ref), custom_call_target="tpu_custom_call" | custom-call | tf_op jit(solution)/shard_map/scatter_owners/pallas_call | solution.py:266
  136.5 0.0 copy-done.3
  136.5 0.0 copy-start.4
  136.6 0.7 copy.19
  137.3 0.3 copy-done.4
  137.6 0.7 copy.20
  138.3 0.0 copy-done.2
  138.3 0.0 copy-start.1
  138.3 1.0 copy.21
  139.3 0.6 copy-done.1
  139.9 0.0 copy-start
  139.9 1.0 copy.22
  140.9 0.6 copy-done
  141.5 1.0 copy.23
Async XLA Ops:
  103.8 32.7 %copy-start.3 = (bf16[128,1024]{1,0:T(8,128)(2,1)S(1)}, bf16[128,1024]{1,0:T(8,128)(2,1)}, u32[]{:S(2)}) copy-start(bf16[128,1024]{1,0:T(8,128)(2,1)} %get-tuple-element.18.right_ref) | copy-start | bytes 786436
  103.8 34.5 %copy-start.2 = (f32[1024,256]{1,0:T(8,128)S(1)}, f32[1024,256]{1,0:T(8,128)}, u32[]{:S(2)}) copy-start(f32[1024,256]{1,0:T(8,128)} %get-tuple-element.10) | copy-start | bytes 3145732
  136.5 1.0 copy-start.4
  138.3 1.6 %copy-start.1 = (f32[1024,256]{1,0:T(8,128)S(1)}, f32[1024,256]{1,0:T(8,128)}, u32[]{:S(2)}) copy-start(f32[1024,256]{1,0:T(8,128)} %get-tuple-element.11) | copy-start | bytes 3145732
  139.9 1.6 %copy-start = (f32[512,512]{1,0:T(8,128)S(1)}, f32[512,512]{1,0:T(8,128)}, u32[]{:S(2)}) copy-start(f32[512,512]{1,0:T(8,128)} %get-tuple-element.12) | copy-start | bytes 3145732
